TPU v7x, 32 devices: a whole 2x2x4 slice. The times are simulated.
32 devices in a mesh: leaf: 8 (over y, x, core), front: 4 (over z).
Axes of the slice: x: 2, y: 2, z: 4, core: 2. Of those that a mesh axis runs over, the one named last changes fastest.
Arguments:
- leaf_rhs: float32 [8, 64, 256], P('leaf', None, 'front'), may hold values from -6 to 6
- sep_rhs: float32 [8, 64, 256], P('leaf', None, 'front'), may hold values from -6 to 6
- leaf_inverse: float32 [8, 256, 256], P('leaf', 'front'), as said below
- sep_inverse: float32 [8, 256, 256], P('leaf', 'front')
- leaf_block: float32 [8, 32, 256], P('leaf', None, 'front'), may hold values from -0.375 to 0.375
- sep_block: float32 [8, 32, 256], P('leaf', None, 'front'), may hold values from -0.375 to 0.375
- pattern: int32 [2, 8, 32], replicated, may hold values from 0 to 255, as said below
- outer_solution: float32 [64, 256], P(None, 'front'), may hold values from -6 to 6
Outputs:
- solution: float32 [2, 8, 64, 256], P(None, 'leaf', None, 'front')
Inputs may be any that keep to these rules, and one draw needn't show every extreme that they name: `pattern`: within one supernode the 32 entries are distinct and rising, the first is 0 and the last is 255. `leaf_inverse`: each leaf block is lower triangular with its diagonal bounded away from zero.
All inputs are finite; a program needn't handle non-finite values.
Results may differ from a plain program's by a relative error of at most 0.0003.
Values sent between devices are 32-bit elements; how exact they have to be, the bound alone decides.
No kernel may reach another device: no remote copies, remote signals or barrier semaphores. Data moves between devices by JAX's collectives and lax.ppermute only.
A program may use at most 64 MiB of HBM per device.

v0:
```python
import jax
import jax.numpy as jnp
from jax import lax
from jax.sharding import PartitionSpec as P


def partner(block, axis, distance):
    count = lax.axis_size(axis)
    route = []
    for low in range(count):
        high = low | 1 << distance
        if high != low and high < count:
            route += [(low, high), (high, low)]
    return lax.ppermute(block, axis, route)


def times_rows(vectors, matrix):
    return jnp.dot(
        vectors, matrix, precision=lax.Precision.HIGHEST, preferred_element_type=jnp.float32
    )


def against_rows(vectors, matrix):
    return lax.dot_general(
        vectors,
        matrix,
        (((1,), (1,)), ((), ())),
        precision=lax.Precision.HIGHEST,
        preferred_element_type=jnp.float32,
    )


def body(
    leaf_rhs, sep_rhs, leaf_inverse, sep_inverse, leaf_block, sep_block, pattern, outer_solution
):
    group_count = lax.axis_size("leaf")
    depth = group_count.bit_length() - 1
    group_pos = lax.axis_index("leaf")
    front_pos = lax.axis_index("front")
    local_rows = leaf_rhs.shape[-1]
    full_rows = leaf_inverse.shape[-1]
    vector_count = leaf_rhs.shape[1]
    leaf_r = leaf_rhs[0]
    leaf_inv = leaf_inverse[0]
    leaf_u = leaf_block[0]
    sep_r = sep_rhs[0]
    sep_inv = sep_inverse[0]
    sep_u = sep_block[0]
    all_rows = jnp.arange(full_rows, dtype=jnp.int32)

    def geometry(level):
        blocks = 2 ** min(level, depth)
        share = local_rows // blocks
        offset = local_rows - (local_rows >> level - 1)
        return (share, offset, group_pos % blocks)

    def label_of(level):
        if level > depth:
            return jnp.int32(0)
        return group_pos // 2**level * 2**level + 2 ** (level - 1)

    def ids_of(level):
        return lax.dynamic_index_in_dim(pattern[1], label_of(level), 0, keepdims=False)

    def block_sum(term, level):
        nbits = min(level, depth)
        if nbits == depth:
            return lax.psum(term, ("leaf", "front"))
        piece = lax.psum_scatter(term, "front", scatter_dimension=1, tiled=True)
        for bit in range(nbits):
            piece = piece + partner(piece, "leaf", bit)
        return lax.all_gather(piece, "front", axis=1, tiled=True)

    leaf_y = against_rows(lax.all_gather(leaf_r, "front", axis=1, tiled=True), leaf_inv)
    leaf_ids = lax.dynamic_index_in_dim(pattern[0], group_pos, 0, keepdims=False)
    child_part = against_rows(leaf_y, leaf_u)
    child_ids = leaf_ids
    solved = {}
    for level in range(1, depth + 2):
        share, offset, inner_pos = geometry(level)
        own_r = sep_r[:, offset : offset + share]
        start_col = front_pos * local_rows + inner_pos * share
        contribution = jnp.zeros((vector_count, full_rows), jnp.float32)
        contribution = lax.dynamic_update_slice(contribution, own_r, (jnp.int32(0), start_col))
        selector = (child_ids[:, None] == all_rows[None, :]).astype(jnp.float32)
        contribution = contribution - times_rows(child_part, selector)
        whole_v = block_sum(contribution, level)
        y_level = against_rows(whole_v, sep_inv[offset : offset + share, :])
        solved[level] = y_level
        if level <= depth:
            child_part = against_rows(y_level, sep_u[:, offset : offset + share])
            child_ids = ids_of(level)
    parent_x = lax.all_gather(outer_solution, "front", axis=1, tiled=True)
    sep_full = jnp.zeros((vector_count, full_rows), jnp.float32)
    for level in range(depth + 1, 0, -1):
        share, offset, inner_pos = geometry(level)
        picked = jnp.take(parent_x, ids_of(level), axis=1)
        rest = solved[level] - times_rows(picked, sep_u[:, offset : offset + share])
        term = times_rows(rest, sep_inv[offset : offset + share, :])
        parent_x = block_sum(term, level)
        sep_full = jnp.where(label_of(level) == group_pos, parent_x, sep_full)
    picked = jnp.take(parent_x, leaf_ids, axis=1)
    rest = leaf_y - times_rows(picked, leaf_u)
    leaf_x = lax.psum_scatter(times_rows(rest, leaf_inv), "front", scatter_dimension=1, tiled=True)
    sep_x = lax.dynamic_slice_in_dim(sep_full, front_pos * local_rows, local_rows, 1)
    return jnp.stack([leaf_x, sep_x])[:, None]


def solution(mesh):
    placed = (
        P("leaf", None, "front"),
        P("leaf", None, "front"),
        P("leaf", "front", None),
        P("leaf", "front", None),
        P("leaf", None, "front"),
        P("leaf", None, "front"),
        P(),
        P(None, "front"),
    )
    return jax.shard_map(
        body, mesh=mesh, in_specs=placed, out_specs=P(None, "leaf", None, "front"), check_vma=False
    )
```

profile of v0, /device:TPU:0, one launch (start us, length us, event | category | flops | bytes accessed | tf_op | source)
XLA Modules:
  0.0 694.5 jit_solution(14276887811836147891)
XLA Ops:
  6.6 0.7 copy-done.9
  7.4 15.1 %all-gather = f32[1,64,256]{1,0,2:T(1,128)S(1)} all-gather(f32[1,64,64]{1,0,2:T(1,128)S(1)} %copy.15), channel_id=2, replica_groups=mesh['leaf'=8,'front'=4] {'front'}, dimensions={2}, use_global_device_ids=true | all-gather | bytes 81920 | tf_op jit(solution)/shard_map/all_gather | solution.py:74
  22.5 0.4 fusion.1
  22.9 0.3 copy-done.6
  23.4 0.7 copy-done.1
  24.1 0.4 dynamic_update_slice.12
  24.8 0.7 copy.26
  25.6 20.6 %reduce-scatter.16.cloned.1.call-done = f32[64,64]{1,0:T(8,128)} async-done(((f32[256,64]{1,0:T(8,128)}), f32[64,64]{1,0:T(8,128)}) %reduce-scatter.16.cloned.1.call-update) | async-done | bytes 16400
  46.2 0.8 copy.27
  47.2 0.4 dynamic_update_slice.13
  47.7 0.6 collective-permute-done
  48.4 13.5 %all_gather.19 = f32[64,256]{0,1:T(8,128)S(1)} all-gather(f32[64,64]{0,1:T(8,128)S(1)} %copy.16), channel_id=1, replica_groups=mesh['leaf'=8,'front'=4] {'front'}, dimensions={1}, use_global_device_ids=true | all-gather | bytes 81920 | tf_op jit(solution)/shard_map/all_gather | solution.py:72
  62.1 0.5 copy-done.2
  63.1 0.7 copy.28
  64.0 17.4 %reduce-scatter.18.cloned.1.call-done = f32[64,64]{1,0:T(8,128)} async-done(((f32[256,64]{1,0:T(8,128)}), f32[64,64]{1,0:T(8,128)}) %reduce-scatter.18.cloned.1.call-update) | async-done | bytes 16400
  81.4 0.8 copy.29
  82.3 1.2 collective-permute-done.1
  83.5 1.5 collective-permute-start.2
  85.0 0.4 dynamic_update_slice.14
  85.5 2.0 collective-permute-done.2
  87.5 13.4 %all_gather.20 = f32[64,256]{0,1:T(8,128)S(1)} all-gather(f32[64,64]{0,1:T(8,128)S(1)} %copy.17), channel_id=1, replica_groups=mesh['leaf'=8,'front'=4] {'front'}, dimensions={1}, use_global_device_ids=true | all-gather | bytes 81920 | tf_op jit(solution)/shard_map/all_gather | solution.py:72
  101.1 0.3 fusion.36
  101.4 0.9 convolution_subtract_fusion.1
  102.3 0.4 dynamic_update_slice.15
  102.8 115.3 %all-reduce.5.cloned.1.call-done = f32[64,256]{1,0:T(8,128)} async-done(((f32[64,256]{1,0:T(8,128)}), f32[64,256]{1,0:T(8,128)}) %all-reduce.5.cloned.1.call-update) | async-done | bytes 65552 | tf_op jit(solution)/shard_map/psum | solution.py:68
  218.1 1.0 fusion.49
  219.0 0.3 fusion.33
  219.3 0.9 convolution_subtract_fusion
  220.3 0.7 copy-done.8
  221.0 14.3 %all_gather.21 = f32[64,256]{0,1:T(8,128)S(1)} all-gather(f32[64,64]{0,1:T(8,128)S(1)} %copy.18), channel_id=1, replica_groups=mesh['leaf'=8,'front'=4] {'front'}, dimensions={1}, use_global_device_ids=true | all-gather | bytes 81920 | tf_op jit(solution)/shard_map/all_gather | solution.py:93
  235.4 0.6 gather_fusion
  235.9 105.9 %all-reduce.7.cloned.1.call-done = f32[64,256]{1,0:T(8,128)} async-done(((f32[64,256]{1,0:T(8,128)}), f32[64,256]{1,0:T(8,128)}) %all-reduce.7.cloned.1.call-update) | async-done | bytes 65552 | tf_op jit(solution)/shard_map/psum | solution.py:68
  341.9 1.0 fusion.45
  342.9 0.3 convolution_subtract_fusion.5
  343.2 0.8 fusion.43
  344.1 121.5 %all-reduce.9.cloned.1.call-done = f32[64,256]{1,0:T(8,128)} async-done(((f32[64,256]{1,0:T(8,128)}), f32[64,256]{1,0:T(8,128)}) %all-reduce.9.cloned.1.call-update) | async-done | bytes 65552 | tf_op jit(solution)/shard_map/psum | solution.py:68
  465.6 0.9 copy.19
  466.6 0.6 gather_fusion.1
  467.2 0.3 convolution_subtract_fusion.8
  467.4 0.9 fusion.47
  468.4 121.0 %all-reduce.11.cloned.1.call-done = f32[64,256]{1,0:T(8,128)} async-done(((f32[64,256]{1,0:T(8,128)}), f32[64,256]{1,0:T(8,128)}) %all-reduce.11.cloned.1.call-update) | async-done | bytes 65552 | tf_op jit(solution)/shard_map/psum | solution.py:68
  589.4 0.9 copy.20
  590.4 0.6 gather_fusion.2
  591.0 0.3 convolution_subtract_fusion.7
  591.2 1.1 convolution_bitcast_fusion.2
  592.4 20.0 %reduce-scatter.20.cloned.1.call-done = f32[64,64]{1,0:T(8,128)} async-done(((f32[256,64]{1,0:T(8,128)}), f32[64,64]{1,0:T(8,128)}) %reduce-scatter.20.cloned.1.call-update) | async-done | bytes 16400
  612.4 0.8 copy.31
  613.3 1.2 collective-permute-done.3
  614.5 1.6 collective-permute-start.4
  616.0 2.3 collective-permute-done.4
  618.5 13.3 %all_gather.22 = f32[64,256]{0,1:T(8,128)S(1)} all-gather(f32[64,64]{0,1:T(8,128)S(1)} %copy.21), channel_id=1, replica_groups=mesh['leaf'=8,'front'=4] {'front'}, dimensions={1}, use_global_device_ids=true | all-gather | bytes 81920 | tf_op jit(solution)/shard_map/all_gather | solution.py:72
  631.8 0.6 gather_fusion.3
  632.6 1.0 convolution_bitcast_fusion.1
  633.8 17.6 %reduce-scatter.22.cloned.1.call-done = f32[64,64]{1,0:T(8,128)} async-done(((f32[256,64]{1,0:T(8,128)}), f32[64,64]{1,0:T(8,128)}) %reduce-scatter.22.cloned.1.call-update) | async-done | bytes 16400
  651.3 0.8 copy.33
  652.3 1.1 collective-permute-done.5
  653.5 13.4 %all_gather.23 = f32[64,256]{0,1:T(8,128)S(1)} all-gather(f32[64,64]{0,1:T(8,128)S(1)} %copy.22), channel_id=1, replica_groups=mesh['leaf'=8,'front'=4] {'front'}, dimensions={1}, use_global_device_ids=true | all-gather | bytes 81920 | tf_op jit(solution)/shard_map/all_gather | solution.py:72
  666.9 0.6 gather_fusion.4
  667.5 0.3 convolution_subtract_fusion.4
  667.9 1.0 convolution_bitcast_fusion
  668.9 0.8 copy-done.4
  669.9 16.6 %reduce-scatter.24.cloned.1.call-done = f32[64,64]{1,0:T(8,128)} async-done(((f32[256,64]{1,0:T(8,128)}), f32[64,64]{1,0:T(8,128)}) %reduce-scatter.24.cloned.1.call-update) | async-done | bytes 16400
  686.5 0.8 copy.35
  687.3 0.6 maximum_bitcast_fusion
  (79 shorter events, 3.3 us)
Async XLA Ops:
  6.5 15.9 %copy-start = (f32[1,64,256]{2,1,0:T(8,128)S(1)}, f32[1,64,256]{2,1,0:T(8,128)}, u32[]{:S(2)}) copy-start(f32[1,64,256]{2,1,0:T(8,128)} %param.12) | copy-start | bytes 196612
  6.5 0.8 copy-start.7
  6.5 39.7 %reduce-scatter.16.cloned.1.call-start = ((), (), s32[]{:S(2)}) async-start(), calls=%async_computation.9 | async-start | bytes 163840
  6.5 0.7 copy-start.9
  22.5 0.7 copy-start.6
  23.4 0.8 copy-start.1
  25.5 55.9 %reduce-scatter.18.cloned.1.call-start = ((), (), s32[]{:S(2)}) async-start(), calls=%async_computation.10 | async-start | bytes 163840
  47.0 1.3 collective-permute-start
  48.4 13.5 %copy-start.3 = (f32[1,64,256]{2,1,0:T(8,128)S(1)}, f32[1,64,256]{2,1,0:T(8,128)}, u32[]{:S(2)}) copy-start(f32[1,64,256]{2,1,0:T(8,128)} %param.13) | copy-start | bytes 196612
  61.9 0.7 copy-start.2
  63.9 154.2 %all-reduce.5.cloned.1.call-start = ((), (), s32[]{:S(2)}) async-start(), calls=%async_computation.5 | async-start | bytes 131072 | tf_op jit(solution)/shard_map/psum | solution.py:68
  82.2 1.3 collective-permute-start.1
  83.5 3.9 collective-permute-start.2
  102.3 239.6 %all-reduce.7.cloned.1.call-start = ((), (), s32[]{:S(2)}) async-start(), calls=%async_computation.6 | async-start | bytes 131072 | tf_op jit(solution)/shard_map/psum | solution.py:68
  220.2 0.8 copy-start.8
  220.2 245.4 %all-reduce.9.cloned.1.call-start = ((), (), s32[]{:S(2)}) async-start(), calls=%async_computation.7 | async-start | bytes 131072 | tf_op jit(solution)/shard_map/psum | solution.py:68
  344.0 245.4 %all-reduce.11.cloned.1.call-start = ((), (), s32[]{:S(2)}) async-start(), calls=%async_computation.8 | async-start | bytes 131072 | tf_op jit(solution)/shard_map/psum | solution.py:68
  468.4 144.0 %reduce-scatter.20.cloned.1.call-start = ((), (), s32[]{:S(2)}) async-start(), calls=%async_computation.11 | async-start | bytes 163840
  592.3 59.0 %reduce-scatter.22.cloned.1.call-start = ((), (), s32[]{:S(2)}) async-start(), calls=%async_computation.12 | async-start | bytes 163840
  613.2 1.3 collective-permute-start.3
  614.5 3.9 collective-permute-start.4
  633.7 52.8 %reduce-scatter.24.cloned.1.call-start = ((), (), s32[]{:S(2)}) async-start(), calls=%async_computation.13 | async-start | bytes 163840
  652.2 1.3 collective-permute-start.5
  668.9 0.8 copy-start.4
  668.9 0.9 copy-start.5
Sparse Core Ops, SparseCore 0:
  25.6 20.5 reduce-scatter.15
  64.0 17.3 reduce-scatter.17
  102.4 115.6 all-reduce.4
  223.5 118.3 all-reduce.6
  347.3 118.3 all-reduce.8
  471.1 118.3 all-reduce.10
  592.4 19.9 reduce-scatter.19
  633.8 17.4 reduce-scatter.21
  669.1 17.4 reduce-scatter.23
where the time goes:
time: 696 us; the launch traced here: 695 us
  waiting for transfers between devices  565 us (81%)
  blocking collectives  83.1 us (12%)
  local copies, waits for them, and re-layouts  16.8 us (2%)
  between operations  13.6 us (2%)
  matrix products  12.1 us (2%)
    psum x4, waiting for transfers between devices, block_sum(): return lax.psum(term, ('leaf', 'front'))  464 us
    unnamed x14, waiting for transfers between devices  92.4 us
    all_gather x4, blocking collectives, block_sum(): return lax.all_gather(piece, 'front', axis=1, tiled=True)  53.7 us
    all_gather x1, blocking collectives, body(): lax.all_gather(leaf_r, 'front', axis=1, tiled=True)  15.1 us
    all_gather x1, blocking collectives, body(): parent_x = lax.all_gather(outer_solution, 'front', axis=1, tiled=True)  14.3 us
  transfers between devices with their start and end apart: 15, of which 15 were waited for; matrix products, arithmetic and copies ran while one was open for 0% of the time, Pallas kernels for 0%

commit v1 on v0

--- a/solution.py
+++ b/solution.py
@@ -65,7 +65,7 @@
     def block_sum(term, level):
         nbits = min(level, depth)
         if nbits == depth:
-            return lax.psum(term, ("leaf", "front"))
+            return jnp.sum(lax.all_gather(term, ("leaf", "front")), axis=0)
         piece = lax.psum_scatter(term, "front", scatter_dimension=1, tiled=True)
         for bit in range(nbits):
             piece = piece + partner(piece, "leaf", bit)

time: 696 us -> 440 us (0.63)
  waiting for transfers between devices: 565 us -> 305 us
  other arithmetic: 0.85 us -> 8.43 us
    psum x4 -> x0, waiting for transfers between devices: 464 us -> none  [block_sum(): return lax.psum(term, ('leaf', 'front'))]
    all_gather x0 -> x4, waiting for transfers between devices: none -> 206 us  [block_sum(): return jnp.sum(lax.all_gather(term, ('leaf', 'front')), axis=0)]
  transfers between devices with their start and end apart: 15 -> 15, of which waited for: 15 -> 14; matrix products, arithmetic and copies ran while one was open for 0% -> 1% of each run, Pallas kernels for 0% -> 0%
where the time goes in v1:
time: 440 us; the launch traced here: 439 us
  waiting for transfers between devices  305 us (69%)
  blocking collectives  82.1 us (19%)
  local copies, waits for them, and re-layouts  14.1 us (3%)
  between operations  13.7 us (3%)
  matrix products  11.9 us (3%)
  other arithmetic  8.43 us (2%)
    all_gather x4, waiting for transfers between devices, block_sum(): return jnp.sum(lax.all_gather(term, ('leaf', 'front')), axis=0)  206 us
    unnamed x14, waiting for transfers between devices  91.4 us
    all_gather x4, blocking collectives, block_sum(): return lax.all_gather(piece, 'front', axis=1, tiled=True)  53.7 us
    all_gather x1, blocking collectives, body(): lax.all_gather(leaf_r, 'front', axis=1, tiled=True)  15.1 us
    all_gather x1, blocking collectives, body(): parent_x = lax.all_gather(outer_solution, 'front', axis=1, tiled=True)  13.4 us
  transfers between devices with their start and end apart: 15, of which 14 were waited for; matrix products, arithmetic and copies ran while one was open for 1% of the time, Pallas kernels for 0%

profile of v1, /device:TPU:0, one launch (start us, length us, event | category | flops | bytes accessed | tf_op | source)
XLA Modules:
  0.0 438.9 jit_solution(15576504019177610010)
XLA Ops:
  6.6 0.7 fusion.79
  7.3 0.8 copy.15
  8.2 15.1 %all-gather = f32[1,64,256]{1,0,2:T(1,128)S(1)} all-gather(f32[1,64,64]{1,0,2:T(1,128)S(1)} %copy.15), channel_id=2, replica_groups=mesh['leaf'=8,'front'=4] {'front'}, dimensions={2}, use_global_device_ids=true | all-gather | bytes 81920 | tf_op jit(solution)/shard_map/all_gather | solution.py:74
  23.2 0.4 fusion.1
  23.6 0.9 fusion.21
  24.5 1.0 dynamic_update_slice.12
  25.8 0.8 copy.26
  26.7 20.7 %reduce-scatter.16.cloned.1.call-done = f32[64,64]{1,0:T(8,128)} async-done(((f32[256,64]{1,0:T(8,128)}), f32[64,64]{1,0:T(8,128)}) %reduce-scatter.16.cloned.1.call-update) | async-done | bytes 16400
  47.4 0.8 copy.27
  48.3 0.8 slice.98
  49.2 0.4 dynamic_update_slice.13
  49.7 13.5 %all_gather.43 = f32[64,256]{0,1:T(8,128)S(1)} all-gather(f32[64,64]{0,1:T(8,128)S(1)} %copy.16), channel_id=1, replica_groups=mesh['leaf'=8,'front'=4] {'front'}, dimensions={1}, use_global_device_ids=true | all-gather | bytes 81920 | tf_op jit(solution)/shard_map/all_gather | solution.py:72
  63.3 1.0 fusion.7
  64.7 0.8 copy.28
  65.6 17.6 %reduce-scatter.18.cloned.1.call-done = f32[64,64]{1,0:T(8,128)} async-done(((f32[256,64]{1,0:T(8,128)}), f32[64,64]{1,0:T(8,128)}) %reduce-scatter.18.cloned.1.call-update) | async-done | bytes 16400
  83.1 0.8 copy.29
  84.0 1.2 collective-permute-done.1
  85.2 1.5 collective-permute-start.2
  86.8 0.4 dynamic_update_slice.14
  87.2 1.9 collective-permute-done.2
  89.2 13.3 %all_gather.44 = f32[64,256]{0,1:T(8,128)S(1)} all-gather(f32[64,64]{0,1:T(8,128)S(1)} %copy.17), channel_id=1, replica_groups=mesh['leaf'=8,'front'=4] {'front'}, dimensions={1}, use_global_device_ids=true | all-gather | bytes 81920 | tf_op jit(solution)/shard_map/all_gather | solution.py:72
  102.7 0.3 fusion.36
  103.0 0.9 convolution_subtract_fusion.1
  104.0 0.4 dynamic_update_slice.15
  104.4 54.4 %all-gather.10.cloned.1.call-done = f32[2048,256]{1,0:T(8,128)} async-done(((f32[64,256]{1,0:T(8,128)}), f32[2048,256]{1,0:T(8,128)}) %all-gather.10.cloned.1.call-update) | async-done | bytes 2097168 | tf_op jit(solution)/shard_map/all_gather | solution.py:68
  158.8 1.7 reduce_sum.36
  160.7 0.3 fusion.33
  160.9 0.9 convolution_subtract_fusion
  162.0 13.4 %all_gather.49 = f32[64,256]{0,1:T(8,128)S(1)} all-gather(f32[64,64]{0,1:T(8,128)S(1)} %copy.18), channel_id=1, replica_groups=mesh['leaf'=8,'front'=4] {'front'}, dimensions={1}, use_global_device_ids=true | all-gather | bytes 81920 | tf_op jit(solution)/shard_map/all_gather | solution.py:93
  175.4 0.7 compare_and_fusion.4
  176.1 0.6 gather_fusion
  176.6 40.7 %all-gather.12.cloned.1.call-done = f32[2048,256]{1,0:T(8,128)} async-done(((f32[64,256]{1,0:T(8,128)}), f32[2048,256]{1,0:T(8,128)}) %all-gather.12.cloned.1.call-update) | async-done | bytes 2097168 | tf_op jit(solution)/shard_map/all_gather | solution.py:68
  217.3 1.7 reduce_sum.37
  219.2 0.3 convolution_subtract_fusion.5
  219.6 0.8 fusion.43
  220.5 55.4 %all-gather.14.cloned.1.call-done = f32[2048,256]{1,0:T(8,128)} async-done(((f32[64,256]{1,0:T(8,128)}), f32[2048,256]{1,0:T(8,128)}) %all-gather.14.cloned.1.call-update) | async-done | bytes 2097168 | tf_op jit(solution)/shard_map/all_gather | solution.py:68
  275.9 1.7 reduce_sum.38
  277.7 0.6 gather_fusion.1
  278.3 0.3 convolution_subtract_fusion.8
  278.5 0.9 fusion.47
  279.5 55.4 %all-gather.16.cloned.1.call-done = f32[2048,256]{1,0:T(8,128)} async-done(((f32[64,256]{1,0:T(8,128)}), f32[2048,256]{1,0:T(8,128)}) %all-gather.16.cloned.1.call-update) | async-done | bytes 2097168 | tf_op jit(solution)/shard_map/all_gather | solution.py:68
  335.0 1.7 reduce_sum.39
  336.8 0.6 gather_fusion.2
  337.4 0.3 convolution_subtract_fusion.7
  337.6 1.1 convolution_bitcast_fusion.2
  338.8 18.1 %reduce-scatter.20.cloned.1.call-done = f32[64,64]{1,0:T(8,128)} async-done(((f32[256,64]{1,0:T(8,128)}), f32[64,64]{1,0:T(8,128)}) %reduce-scatter.20.cloned.1.call-update) | async-done | bytes 16400
  356.9 0.8 copy.31
  357.8 1.2 collective-permute-done.3
  359.0 1.5 collective-permute-start.4
  360.5 2.4 collective-permute-done.4
  363.0 13.3 %all_gather.54 = f32[64,256]{0,1:T(8,128)S(1)} all-gather(f32[64,64]{0,1:T(8,128)S(1)} %copy.21), channel_id=1, replica_groups=mesh['leaf'=8,'front'=4] {'front'}, dimensions={1}, use_global_device_ids=true | all-gather | bytes 81920 | tf_op jit(solution)/shard_map/all_gather | solution.py:72
  376.3 0.6 gather_fusion.3
  376.9 0.2 convolution_subtract_fusion.6
  377.1 1.1 convolution_bitcast_fusion.1
  378.3 17.5 %reduce-scatter.22.cloned.1.call-done = f32[64,64]{1,0:T(8,128)} async-done(((f32[256,64]{1,0:T(8,128)}), f32[64,64]{1,0:T(8,128)}) %reduce-scatter.22.cloned.1.call-update) | async-done | bytes 16400
  395.8 0.8 copy.33
  396.8 1.1 collective-permute-done.5
  398.0 13.4 %all_gather.55 = f32[64,256]{0,1:T(8,128)S(1)} all-gather(f32[64,64]{0,1:T(8,128)S(1)} %copy.22), channel_id=1, replica_groups=mesh['leaf'=8,'front'=4] {'front'}, dimensions={1}, use_global_device_ids=true | all-gather | bytes 81920 | tf_op jit(solution)/shard_map/all_gather | solution.py:72
  411.4 0.6 gather_fusion.4
  412.0 0.3 convolution_subtract_fusion.4
  412.3 1.0 convolution_bitcast_fusion
  413.5 17.4 %reduce-scatter.24.cloned.1.call-done = f32[64,64]{1,0:T(8,128)} async-done(((f32[256,64]{1,0:T(8,128)}), f32[64,64]{1,0:T(8,128)}) %reduce-scatter.24.cloned.1.call-update) | async-done | bytes 16400
  430.9 0.8 copy.35
  431.8 0.6 maximum_bitcast_fusion
  (75 shorter events, 3.0 us)
Async XLA Ops:
  6.5 16.7 %copy-start = (f32[1,64,256]{2,1,0:T(8,128)S(1)}, f32[1,64,256]{2,1,0:T(8,128)}, u32[]{:S(2)}) copy-start(f32[1,64,256]{2,1,0:T(8,128)} %param.12) | copy-start | bytes 196612
  6.5 80.2 %copy-start.1 = (f32[1,64,64]{2,1,0:T(8,128)S(1)}, f32[1,64,64]{2,1,0:T(8,128)}, u32[]{:S(2)}) copy-start(f32[1,64,64]{2,1,0:T(8,128)} %param.11) | copy-start | bytes 49156
  6.5 96.0 %copy-start.3 = (f32[1,64,256]{2,1,0:T(8,128)S(1)}, f32[1,64,256]{2,1,0:T(8,128)}, u32[]{:S(2)}) copy-start(f32[1,64,256]{2,1,0:T(8,128)} %param.13) | copy-start | bytes 196612
  6.5 57.7 %copy-start.2 = (f32[1,32,64]{2,1,0:T(8,128)S(1)}, f32[1,32,64]{2,1,0:T(8,128)}, u32[]{:S(2)}) copy-start(f32[1,32,64]{2,1,0:T(8,128)} %param.15) | copy-start | bytes 24580
  6.5 40.8 %reduce-scatter.16.cloned.1.call-start = ((), (), s32[]{:S(2)}) async-start(), calls=%async_computation.9 | async-start | bytes 163840
  26.6 56.5 %reduce-scatter.18.cloned.1.call-start = ((), (), s32[]{:S(2)}) async-start(), calls=%async_computation.10 | async-start | bytes 163840
  48.2 1.4 collective-permute-start
  64.7 97.2 %copy-start.5 = (f32[64,64]{1,0:T(8,128)S(1)}, f32[64,64]{1,0:T(8,128)}, u32[]{:S(2)}) copy-start(f32[64,64]{1,0:T(8,128)} %param.17) | copy-start | bytes 49156
  65.5 93.3 %all-gather.10.cloned.1.call-start = ((), (), s32[]{:S(2)}) async-start(), calls=%async_computation.5 | async-start | bytes 2162688 | tf_op jit(solution)/shard_map/all_gather | solution.py:68
  84.0 1.3 collective-permute-start.1
  85.2 3.9 collective-permute-start.2
  103.9 113.4 %all-gather.12.cloned.1.call-start = ((), (), s32[]{:S(2)}) async-start(), calls=%async_computation.6 | async-start | bytes 2162688 | tf_op jit(solution)/shard_map/all_gather | solution.py:68
  161.8 114.1 %all-gather.14.cloned.1.call-start = ((), (), s32[]{:S(2)}) async-start(), calls=%async_computation.7 | async-start | bytes 2162688 | tf_op jit(solution)/shard_map/all_gather | solution.py:68
  220.4 114.6 %all-gather.16.cloned.1.call-start = ((), (), s32[]{:S(2)}) async-start(), calls=%async_computation.8 | async-start | bytes 2162688 | tf_op jit(solution)/shard_map/all_gather | solution.py:68
  279.5 77.4 %reduce-scatter.20.cloned.1.call-start = ((), (), s32[]{:S(2)}) async-start(), calls=%async_computation.11 | async-start | bytes 163840
  335.0 77.0 %copy-start.4 = (f32[1,32,64]{2,1,0:T(8,128)S(1)}, f32[1,32,64]{2,1,0:T(8,128)}, u32[]{:S(2)}) copy-start(f32[1,32,64]{2,1,0:T(8,128)} %param.14) | copy-start | bytes 24580
  338.7 57.1 %reduce-scatter.22.cloned.1.call-start = ((), (), s32[]{:S(2)}) async-start(), calls=%async_computation.12 | async-start | bytes 163840
  357.7 1.3 collective-permute-start.3
  359.0 3.9 collective-permute-start.4
  378.2 52.7 %reduce-scatter.24.cloned.1.call-start = ((), (), s32[]{:S(2)}) async-start(), calls=%async_computation.13 | async-start | bytes 163840
  396.6 1.3 collective-permute-start.5
Sparse Core Ops, SparseCore 0:
  26.7 20.6 reduce-scatter.15
  65.6 17.4 reduce-scatter.17
  104.0 54.7 all-gather.9
  161.9 55.3 all-gather.11
  220.5 55.3 all-gather.13
  279.6 55.3 all-gather.15
  338.8 17.9 reduce-scatter.19
  378.3 17.4 reduce-scatter.21
  413.5 17.3 reduce-scatter.23
